TPU v7x, 128 devices: a whole 4x4x4 slice. The times are simulated.
128 devices in a mesh: rows: 32 (over x, y, core), tok: 4 (over z).
Axes of the slice: x: 4, y: 4, z: 4, core: 2. Of those that a mesh axis runs over, the one named last changes fastest.
Arguments:
- pixels: bfloat16 [4096, 425, 512], P('rows', None, 'tok'), as said below
- scene_starts: int32 [4], replicated, may hold values from 0 to 4032, as said below
- owners: int32 [1024, 128], P('rows', 'tok'), may hold values from 0 to 31, as said below
- start_basis: float32 [425, 64], replicated, may hold values from -6 to 6
Outputs:
- tokens: bfloat16 [131072, 1024], P(('rows', 'tok'))
- noise_scores: bfloat16 [4096, 64, 512], P('rows', None, 'tok')
Inputs may be any that keep to these rules, and one draw needn't show every extreme that they name: `scene_starts`: entry 0 is 0 and the entries rise strictly. `owners`: in each block of 32 x 128/4 patches every owner appears exactly 32 times. `pixels`: finite radiances; the scenes have a positive mean.
All inputs are finite; a program needn't handle non-finite values. Where the computation divides by a largest or mean magnitude, that divisor is 1e-20 or more.
Results may differ from a plain program's by a relative error of at most 0.0068.
Values may be sent and summed in bfloat16 or wider, within the bound.
No kernel may reach another device: no remote copies, remote signals or barrier semaphores. Data moves between devices by JAX's collectives and lax.ppermute only.
A program may use at most 192 MiB of HBM per device.

v0:
```python
import functools

import jax
import jax.numpy as jnp
from jax import lax
from jax.experimental import pallas as pl
from jax.experimental.pallas import tpu as pltpu
from jax.sharding import PartitionSpec as P

B = 425
BP = 432
BW = 512
KC = 64
R = 16
OWN = 32
PATCHES = 1024
TILES = 128
F32 = jnp.float32
BF = jnp.bfloat16
NN = (((1,), (0,)), ((), ()))
NT = (((1,), (1,)), ((), ()))


def lower_gram(acc_ref, a):
    nt=(((1,),(1,)),((),()))
    g=lax.dot_general(a, a[0:256], nt, preferred_element_type=jnp.float32)
    h=lax.dot_general(a[256:432], a[256:432], nt, preferred_element_type=jnp.float32)
    acc_ref[0:432,:]+=g[:,0:128]
    acc_ref[432:736,:]+=g[128:432,128:256]
    acc_ref[736:912,:]+=h[:,0:128]
    acc_ref[912:960,0:48]+=h[128:176,128:176]

def noise_kernel(base_ref, starts_ref, x_ref, halo_ref, xt_ref, acc_ref, scr, prev, dbuf):
    s=pl.program_id(0); n=pl.num_programs(0)
    @pl.when(s==0)
    def _():
        acc_ref[...]=jnp.zeros_like(acc_ref)
        prev[...]=jnp.zeros_like(prev)
        scr[:,B*8:BP*8,:]=jnp.ones((2,(BP-B)*8,128),jnp.float32)
    def valid_after(row):
        nxt=base_ref[0]+row+1
        ok=nxt<4096
        for i in range(4):
            ok=jnp.logical_and(ok, nxt!=starts_ref[i])
        return jnp.logical_and(ok,row>=0)
    for g in range(2):
        scr[g,0:B*8,:]=x_ref[:,g*8:(g+1)*8,:].astype(jnp.float32).reshape(B*8,128)
    for r in range(R):
        cur=scr[r//8, pl.ds(r%8,BP,stride=8),:]
        before=prev[...] if r==0 else scr[(r-1)//8, pl.ds((r-1)%8,BP,stride=8),:]
        keep=valid_after(s*R+r-1)
        d=jnp.where(keep, before-cur, 0.0)
        dbuf[:,r*128:(r+1)*128]=d.astype(jnp.bfloat16)
        xt_ref[r]=cur.astype(jnp.bfloat16)
        if r==R-1: prev[...]=cur
    lower_gram(acc_ref, dbuf[...])
    @pl.when(s==n-1)
    def _():
        keep=valid_after(s*R+R-1)
        d=jnp.where(keep, prev[0:B]-halo_ref[0].astype(jnp.float32), 0.0)
        dd=jnp.concatenate([d,jnp.zeros((BP-B,128),jnp.float32)],0).astype(jnp.bfloat16)
        lower_gram(acc_ref, dd)

def noise_moments(pixels_t, halo, base, starts):
    return pl.pallas_call(noise_kernel,
      grid_spec=pltpu.PrefetchScalarGridSpec(num_scalar_prefetch=2, grid=(128//R,),
        in_specs=[pl.BlockSpec((B,R,128),lambda s,*_:(0,s,0)), pl.BlockSpec((1,B,128),lambda s,*_:(0,0,0))],
        out_specs=[pl.BlockSpec((R,BP,128),lambda s,*_:(s,0,0)), pl.BlockSpec((1024,128),lambda s,*_:(0,0))],
        scratch_shapes=[pltpu.VMEM((2,BP*8,128),jnp.float32), pltpu.VMEM((BP,128),jnp.float32), pltpu.VMEM((BP,R*128),jnp.bfloat16)]),
      out_shape=[jax.ShapeDtypeStruct((128,BP,128),jnp.bfloat16), jax.ShapeDtypeStruct((1024,128),jnp.float32)],
      compiler_params=pltpu.CompilerParams(vmem_limit_bytes=48<<20),
      cost_estimate=pl.CostEstimate(flops=6_000_000_000,bytes_accessed=30_000_000,transcendentals=0), name="noise_moments")(base,starts,pixels_t,halo)

def signal_kernel(xt_ref, acc_ref):
    @pl.when(pl.program_id(0)==0)
    def _(): acc_ref[...]=jnp.zeros_like(acc_ref)
    a=jnp.concatenate([xt_ref[r] for r in range(R)],axis=1)
    lower_gram(acc_ref,a)

def signal_moments(xt):
    return pl.pallas_call(signal_kernel, grid=(128//R,),
      in_specs=[pl.BlockSpec((R,BP,128),lambda s:(s,0,0))],
      out_specs=pl.BlockSpec((1024,128),lambda s:(0,0)),
      out_shape=jax.ShapeDtypeStruct((1024,128),jnp.float32),
      compiler_params=pltpu.CompilerParams(vmem_limit_bytes=48<<20),
      cost_estimate=pl.CostEstimate(flops=6_000_000_000,bytes_accessed=15_000_000,transcendentals=0), name="signal_moments")(xt)

def cut(x):
    hi=x.astype(BF)
    return hi,(x-hi.astype(F32)).astype(BF)

def times(a,b,dims=NN):
    (ah,al),(bh,bl)=a,b
    def mm(x,y): return lax.dot_general(x,y,dims,preferred_element_type=F32)
    return mm(ah,bh)+(mm(ah,bl)+mm(al,bh))

def unpacked(ref, full):
    starts=(0,432,736,912)
    for j in range(4):
        lo=starts[j]; rows=BP-128*j
        full[128*j:BP,128*j:128*(j+1)]=ref[lo:lo+rows,:]
    for j in range(4):
        for i in range(j+1,4):
            full[128*j:128*(j+1),128*i:128*(i+1)]=full[128*i:128*(i+1),128*j:128*(j+1)].T

def triangular_inverse(g):
    row=lax.broadcasted_iota(jnp.int32,(KC,2*KC),0); col=lax.broadcasted_iota(jnp.int32,(KC,2*KC),1)
    m=jnp.concatenate([g,jnp.zeros((KC,KC),F32)],axis=1)+jnp.where(col==row+KC,1.0,0.0)
    for j in range(KC):
        line=m[j:j+1,:]
        pivot=m[j:j+1,j:j+1]
        f=m[:,j:j+1]*(1.0/pivot)
        f=jnp.where(row>j,f,0.0)
        scaled=line*lax.rsqrt(pivot)
        m=jnp.where(row==j,scaled,m-f*line)
    return m[:,KC:]

def orthonormal(y):
    yc=cut(y)
    yt=y.T
    g=times(cut(yt),yc)
    li=triangular_inverse(g)
    return times(yc,cut(li),NT)

def put(ref,i,x):
    h,l=cut(x)
    ref[i,0,0:BP,:]=h; ref[i,1,0:BP,:]=l
def got(ref,i,rows=BW): return ref[i,0,0:rows,:],ref[i,1,0:rows,:]

def whiten_kernel(n_ref, w_ref, full, cuts, lf, *, norm, iters=10):
    full[...]=jnp.zeros_like(full)
    cuts[...]=jnp.zeros_like(cuts)
    unpacked(n_ref, full)
    row=lax.broadcasted_iota(jnp.int32,(BP,BW),0); col=lax.broadcasted_iota(jnp.int32,(BP,BW),1)
    inside=jnp.logical_and(row<B,col<B)
    cov=jnp.where(inside, full[0:BP,:]*(1.0/norm), 0.0)
    scale=jnp.max(jnp.sum(jnp.abs(cov),axis=1,keepdims=True),axis=0,keepdims=True)
    eye=jnp.where(jnp.logical_and(row==col,row<B),1.0,0.0)
    z=cov/scale
    full[0:BP,:]=z
    put(cuts,0,z)
    low=1.5*eye-0.5*z
    lf[...]=low
    put(cuts,1,low)
    for k in range(iters-1):
        w=1.5*z-0.5*times(got(cuts,0,BP),got(cuts,0))
        put(cuts,2,w)
        z=1.5*w-0.5*times(got(cuts,0,BP),got(cuts,2))
        full[0:BP,:]=z
        put(cuts,0,z)
        low=1.5*low-0.5*times(got(cuts,0,BP),got(cuts,1))
        put(cuts,1,low)
    w_ref[...]=low*lax.rsqrt(scale)

def whiten(tiles,norm):
    return pl.pallas_call(functools.partial(whiten_kernel,norm=norm),
      out_shape=jax.ShapeDtypeStruct((BP,BW),F32),
      scratch_shapes=[pltpu.VMEM((BW,BW),F32),pltpu.VMEM((3,2,BW,BW),BF),pltpu.VMEM((BP,BW),F32)],
      compiler_params=pltpu.CompilerParams(vmem_limit_bytes=40<<20),
      cost_estimate=pl.CostEstimate(flops=15_000_000_000,bytes_accessed=2_000_000,transcendentals=0),name="whiten")(tiles)

def start_kernel(b_ref,o_ref,pad):
    pad[...]=jnp.zeros_like(pad)
    pad[0:B,:]=b_ref[...]
    o_ref[...]=orthonormal(pad[...])

def start_orth(b):
    return pl.pallas_call(start_kernel,out_shape=jax.ShapeDtypeStruct((BP,KC),F32),scratch_shapes=[pltpu.VMEM((BP,KC),F32)],
      compiler_params=pltpu.CompilerParams(vmem_limit_bytes=40<<20),
      cost_estimate=pl.CostEstimate(flops=100_000_000,bytes_accessed=2_000_000,transcendentals=0),name="start_orth")(b)

def subspace_kernel(s_ref,w_ref,q_ref,pt_ref,full,cuts,thin,*,total):
    full[...]=jnp.zeros_like(full)
    cuts[...]=jnp.zeros_like(cuts)
    thin[...]=jnp.zeros_like(thin)
    unpacked(s_ref,full)
    row=lax.broadcasted_iota(jnp.int32,(BP,BW),0); col=lax.broadcasted_iota(jnp.int32,(BP,BW),1)
    inside=jnp.logical_and(row<B,col<B)
    mrow=full[B:B+1,:]*(1.0/total)
    mcol=full[0:BP,B:B+1]*(1.0/total)
    cov=jnp.where(inside,full[0:BP,:]*(1.0/total)-mcol*mrow,0.0)
    put(cuts,0,cov)
    put(cuts,1,w_ref[...])
    put(cuts,2,times(got(cuts,1,BP),got(cuts,0)))
    put(cuts,0,times(got(cuts,2,BP),got(cuts,1)))
    def thin_cut(x):
        h,l=cut(x); thin[0,0:BP,:]=h; thin[1,0:BP,:]=l
        return thin[0],thin[1]
    q=q_ref[...]
    for _ in range(2):
        q=orthonormal(times(got(cuts,0,BP),thin_cut(q)))
    p=times(got(cuts,1,BP),thin_cut(q)).astype(BF)
    pt=p.astype(F32).T
    off=-jnp.sum(pt*mrow[:,0:BP],axis=1,keepdims=True)
    lane=lax.broadcasted_iota(jnp.int32,(KC,BP),1)
    o1=off.astype(BF).astype(F32); o2=(off-o1).astype(BF).astype(F32); o3=off-o1-o2
    pt=jnp.where(lane<B,pt,jnp.where(lane==B,o1,jnp.where(lane==B+1,o2,jnp.where(lane==B+2,o3,0.0))))
    pt_ref[...]=pt.astype(BF)

def subspace(tiles,w,q,total):
    return pl.pallas_call(functools.partial(subspace_kernel,total=total),
      out_shape=jax.ShapeDtypeStruct((KC,BP),BF),
      scratch_shapes=[pltpu.VMEM((BW,BW),F32),pltpu.VMEM((3,2,BW,BW),BF),pltpu.VMEM((2,BW,KC),BF)],
      compiler_params=pltpu.CompilerParams(vmem_limit_bytes=40<<20),
      cost_estimate=pl.CostEstimate(flops=3_000_000_000,bytes_accessed=2_000_000,transcendentals=0),name="subspace")(tiles,w,q)

def order_kernel(o_ref, perm_ref):
    own=o_ref[...]
    hot=lax.broadcasted_iota(jnp.int32,(OWN,PATCHES),0)==own
    before=(lax.broadcasted_iota(jnp.int32,(PATCHES,PATCHES),0)<lax.broadcasted_iota(jnp.int32,(PATCHES,PATCHES),1))
    rank=lax.dot_general(hot.astype(F32).astype(BF),before.astype(F32).astype(BF),NN,preferred_element_type=F32)
    rank=jnp.sum(jnp.where(hot,rank,0.0),axis=0,keepdims=True)
    place=own*(PATCHES//OWN)+rank.astype(jnp.int32)
    perm_ref[...]=(lax.broadcasted_iota(jnp.int32,(PATCHES,PATCHES),0)==place).astype(F32).astype(BF)

def owner_order(own):
    return pl.pallas_call(order_kernel,out_shape=jax.ShapeDtypeStruct((PATCHES,PATCHES),BF),
      compiler_params=pltpu.CompilerParams(vmem_limit_bytes=40<<20),
      cost_estimate=pl.CostEstimate(flops=100_000_000,bytes_accessed=2_000_000,transcendentals=0),name="owner_order")(own)

def token_kernel(pt_ref,x_ref,perm_ref,out_ref,tok):
    s=pl.program_id(0); n=pl.num_programs(0)
    a=lax.broadcasted_iota(jnp.int32,(128,128),0); c=lax.broadcasted_iota(jnp.int32,(128,128),1)
    pick=((a%32)*4+a//32==c).astype(F32).astype(BF)
    pt=pt_ref[...]
    for p in range(R//4):
        ys=[]
        for h in range(2):
            r=4*p+2*h
            rhs=jnp.concatenate([x_ref[r],x_ref[r+1]],axis=1)
            y=lax.dot_general(pt,rhs,NN,preferred_element_type=F32).astype(BF)
            ys+=[y[:,0:128],y[:,128:256]]
        y=jnp.concatenate(ys,axis=0)
        t=lax.dot_general(pick,y,NT,preferred_element_type=F32)
        parts=[t[32*j:32*(j+1),64*i:64*(i+1)] for i in range(4) for j in range(4)]
        tok[pl.ds(pl.multiple_of(s*(R//4)*32+p*32,32),32),:]=jnp.concatenate(parts,axis=1).astype(BF)
    @pl.when(s==n-1)
    def _():
        for m in range(4):
            out_ref[256*m:256*(m+1),:]=lax.dot_general(perm_ref[256*m:256*(m+1),:],tok[...],NN,preferred_element_type=F32).astype(BF)

def token_blocks(pt,xt,perm):
    return pl.pallas_call(token_kernel,grid=(128//R,),
      in_specs=[pl.BlockSpec((KC,BP),lambda s:(0,0)),pl.BlockSpec((R,BP,128),lambda s:(s,0,0)),pl.BlockSpec((PATCHES,PATCHES),lambda s:(0,0))],
      out_specs=pl.BlockSpec((PATCHES,1024),lambda s:(0,0)),
      out_shape=jax.ShapeDtypeStruct((PATCHES,1024),BF),
      scratch_shapes=[pltpu.VMEM((PATCHES,1024),BF)],
      compiler_params=pltpu.CompilerParams(vmem_limit_bytes=48<<20),
      cost_estimate=pl.CostEstimate(flops=4_000_000_000,bytes_accessed=18_000_000,transcendentals=0),name="token_blocks")(pt,xt,perm)

def score_kernel(base_ref,starts_ref,pt_ref,x_ref,next_ref,halo_ref,out_ref):
    s=pl.program_id(0); n=pl.num_programs(0)
    pt=pt_ref[...]
    def differ(r):
        cur=x_ref[r].astype(F32)
        if r<R-1: ahead=x_ref[r+1].astype(F32)
        else:
            halo=jnp.concatenate([halo_ref[0].astype(F32),jnp.ones((BP-B,128),F32)],axis=0)
            ahead=jnp.where(s==n-1,halo,next_ref[0].astype(F32))
        nxt=base_ref[0]+s*R+r+1
        ok=nxt<4096
        for i in range(4): ok=jnp.logical_and(ok,nxt!=starts_ref[i])
        return jnp.where(ok,cur-ahead,0.0).astype(BF)
    for h in range(R//2):
        y=lax.dot_general(pt,jnp.concatenate([differ(2*h),differ(2*h+1)],axis=1),NN,preferred_element_type=F32).astype(BF)
        out_ref[2*h]=y[:,0:128]; out_ref[2*h+1]=y[:,128:256]

def scores(pt,xt,halo,base,starts):
    n=128//R
    return pl.pallas_call(score_kernel,
      grid_spec=pltpu.PrefetchScalarGridSpec(num_scalar_prefetch=2,grid=(n,),
        in_specs=[pl.BlockSpec((KC,BP),lambda s,*_:(0,0)),pl.BlockSpec((R,BP,128),lambda s,*_:(s,0,0)),
          pl.BlockSpec((1,BP,128),lambda s,*_:(jnp.minimum((s+1)*R,127),0,0)),pl.BlockSpec((1,B,128),lambda s,*_:(0,0,0))],
        out_specs=pl.BlockSpec((R,KC,128),lambda s,*_:(s,0,0))),
      out_shape=jax.ShapeDtypeStruct((128,KC,128),BF),
      compiler_params=pltpu.CompilerParams(vmem_limit_bytes=48<<20),
      cost_estimate=pl.CostEstimate(flops=4_000_000_000,bytes_accessed=18_000_000,transcendentals=0),name="noise_scores")(base,starts,pt,xt,xt,halo)


def local(pixels, scene_starts, owners, start_basis):
    rows = lax.axis_size("rows")
    cols = lax.axis_size("tok")
    local_rows = pixels.shape[0]
    both = ("rows", "tok")
    halo = lax.ppermute(pixels[0:1], "rows", [(r, r - 1) for r in range(1, rows)])
    base = (lax.axis_index("rows") * local_rows).astype(jnp.int32).reshape(1)
    total = float(rows * local_rows * cols * pixels.shape[2])
    norm = 2.0 * (rows * local_rows - scene_starts.shape[0]) * cols * pixels.shape[2]
    banded, noise_part = noise_moments(jnp.transpose(pixels, (1, 0, 2)), halo, base, scene_starts)
    noise_own = lax.all_to_all(noise_part.reshape(TILES, 8, 128), both, 0, 0, tiled=True).sum(axis=0)
    signal_part = signal_moments(banded)
    mixed = jnp.concatenate(
        [jnp.broadcast_to(noise_own, (TILES, 8, 128)), signal_part.reshape(TILES, 8, 128)], axis=1
    )
    mixed = lax.all_to_all(mixed, both, 0, 0, tiled=True)
    noise = mixed[:, 0:8].reshape(TILES * 8, 128)
    signal_own = mixed[:, 8:16].sum(axis=0)
    perm = owner_order(owners.reshape(1, PATCHES))
    basis = start_orth(start_basis)
    signal = lax.all_to_all(jnp.broadcast_to(signal_own, (TILES, 8, 128)), both, 0, 0, tiled=True)
    whitener = whiten(noise, norm)
    projector = subspace(signal.reshape(TILES * 8, 128), whitener, basis, total)
    outgoing = token_blocks(projector, banded, perm)
    arrived = lax.all_to_all(outgoing.reshape(OWN, PATCHES // OWN, 1024), "rows", 0, 0, tiled=True)
    noise_scores = scores(projector, banded, halo, base, scene_starts)
    return arrived.reshape(PATCHES, 1024), noise_scores


def solution(mesh):
    return jax.shard_map(
        local,
        mesh=mesh,
        in_specs=(P("rows", None, "tok"), P(), P("rows", "tok"), P()),
        out_specs=(P(("rows", "tok"), None), P("rows", None, "tok")),
        check_vma=False,
    )
```

profile of v0, /device:TPU:1, one launch (start us, length us, event | category | flops | bytes accessed | tf_op | source)
XLA Modules:
  0.0 180.3 jit_solution(6840366581672786056)
XLA Ops:
  0.6 1.3 slice.9
  1.9 3.3 %collective-permute-start = (bf16[1,425,128]{2,1,0:T(8,128)(2,1)S(1)}, bf16[1,425,128]{2,1,0:T(8,128)(2,1)S(1)}, u32[]{:S(2)}, u32[]{:S(2)}) collective-permute-start(bf16[1,425,128]{2,1,0:T(8,128)(2,1)S(1)} %copy.8), channel_id=1, source_target_pairs={{4,0},{8,4},{12,8},{16,12},{20,16},{24,20},{28,24},{32,28},{36,32}... | collective-permute-start | bytes 326408 | tf_op jit(solution)/shard_map/ppermute | solution.py:285
  5.2 3.7 %collective-permute-done.halo_ref = bf16[1,425,128]{2,1,0:T(8,128)(2,1)S(1)} collective-permute-done((bf16[1,425,128]{2,1,0:T(8,128)(2,1)S(1)}, bf16[1,425,128]{2,1,0:T(8,128)(2,1)S(1)}, u32[]{:S(2)}, u32[]{:S(2)}) %collective-permute-start) | collective-permute-done | bytes 108832 | tf_op jit(solution)/shard_map/ppermute | solution.py:285
  8.9 0.7 copy-done.1
  9.6 19.1 %noise_moments.1 = (bf16[128,432,128]{2,1,0:T(8,128)(2,1)}, f32[1024,128]{1,0:T(8,128)}) custom-call(s32[1]{0:T(128)} %bitcast.base_ref, s32[4]{0:T(128)S(1)} %copy-done.1, bf16[425,128,128]{2,1,0:T(8,128)(2,1)} %bitcast.13, bf16[1,425,128]{2,1,0:T(8,128)(2,1)S(1)} %collective-permute-done.halo_ref), custom_call_target="tpu_custom_call" | custom-call | flops 6000000000 | bytes 30000000 | tf_op jit(solution)/shard_map/noise_moments/pallas_call | solution.py:65
  28.7 11.9 %all-to-all-start = ((f32[128,8,128]{2,1,0:T(8,128)}), f32[128,8,128]{2,1,0:T(8,128)S(1)}, u32[]{:S(2)}, u32[]{:S(2)}) async-start(f32[128,8,128]{2,1,0:T(8,128)} %bitcast.2), calls=%async_computation | async-start | bytes 1048576 | tf_op jit(solution)/shard_map/all_to_all | solution.py:290
  40.6 10.6 %signal_moments.1 = f32[1024,128]{1,0:T(8,128)S(1)} custom-call(bf16[128,432,128]{2,1,0:T(8,128)(2,1)} %get-tuple-element.5.xt_ref.x_ref.next_ref), custom_call_target="tpu_custom_call" | custom-call | flops 6000000000 | bytes 15000000 | tf_op jit(solution)/shard_map/signal_moments/pallas_call | solution.py:81
  51.3 3.3 %all-to-all-done = f32[128,8,128]{2,1,0:T(8,128)S(1)} async-done(((f32[128,8,128]{2,1,0:T(8,128)}), f32[128,8,128]{2,1,0:T(8,128)S(1)}, u32[]{:S(2)}, u32[]{:S(2)}) %all-to-all-start) | async-done | bytes 524320 | tf_op jit(solution)/shard_map/all_to_all | solution.py:290
  54.5 0.1 reduce_sum.18
  54.7 0.0 copy-start.5
  54.7 0.0 copy-start.6
  54.7 1.0 pad_maximum_fusion
  55.8 7.0 %all-to-all-start.1 = ((f32[128,16,128]{2,1,0:T(8,128)}), f32[128,16,128]{2,1,0:T(8,128)}, u32[]{:S(2)}, u32[]{:S(2)}) async-start(f32[128,16,128]{2,1,0:T(8,128)} %pad_maximum_fusion), calls=%async_computation.1 | async-start | bytes 2097152 | tf_op jit(solution)/shard_map/all_to_all | solution.py:295
  62.8 0.1 copy.7.b_ref
  62.9 0.1 reshape.33.o_ref
  63.0 6.0 %start_orth.1.q_ref = f32[432,64]{1,0:T(8,128)S(1)} custom-call(f32[425,64]{1,0:T(8,128)S(1)} %copy.7.b_ref), custom_call_target="tpu_custom_call" | custom-call | flops 100000000 | bytes 2000000 | tf_op jit(solution)/shard_map/start_orth/pallas_call | solution.py:168
  69.0 1.3 owner_order.1.perm_ref
  70.3 11.6 %all-to-all-done.1 = f32[128,16,128]{2,1,0:T(8,128)} async-done(((f32[128,16,128]{2,1,0:T(8,128)}), f32[128,16,128]{2,1,0:T(8,128)}, u32[]{:S(2)}, u32[]{:S(2)}) %all-to-all-start.1) | async-done | bytes 1048608 | tf_op jit(solution)/shard_map/all_to_all | solution.py:295
  81.9 1.3 slice_bitcast_fusion
  83.3 0.8 broadcast_in_dim.7
  84.1 4.1 %all-to-all-start.2 = ((f32[128,8,128]{2,1,0:T(8,128)}), f32[128,8,128]{2,1,0:T(8,128)S(1)}, u32[]{:S(2)}, u32[]{:S(2)}) async-start(f32[128,8,128]{2,1,0:T(8,128)} %broadcast_in_dim.7), calls=%async_computation.2 | async-start | bytes 1048576 | tf_op jit(solution)/shard_map/all_to_all | solution.py:300
  88.2 20.7 %whiten.1.w_ref = f32[432,512]{1,0:T(8,128)S(1)} custom-call(f32[1024,128]{1,0:T(8,128)S(1)} %get-tuple-element.6.n_ref), custom_call_target="tpu_custom_call" | custom-call | flops 15000000512 | bytes 2000000 | tf_op jit(solution)/shard_map/whiten/pallas_call | solution.py:156
  108.9 0.0 copy-start.3
  108.9 0.9 copy-done.3
  109.8 1.2 copy-done.4
  111.0 16.8 %subspace.1.pt_ref = bf16[64,432]{1,0:T(8,128)(2,1)S(1)} custom-call(f32[1024,128]{1,0:T(8,128)S(1)} %bitcast.10, f32[432,512]{1,0:T(8,128)S(1)} %copy-done.4, f32[432,64]{1,0:T(8,128)S(1)} %start_orth.1.q_ref), custom_call_target="tpu_custom_call" | custom-call | flops 3000000000 | bytes 2000000 | tf_op jit(solution)/shard_map/subspace/pallas_call | solution.py:201
  127.8 14.0 %token_blocks.1 = bf16[1024,1024]{1,0:T(8,128)(2,1)S(1)} custom-call(bf16[64,432]{1,0:T(8,128)(2,1)S(1)} %subspace.1.pt_ref, bf16[128,432,128]{2,1,0:T(8,128)(2,1)} %get-tuple-element.5.xt_ref.x_ref.next_ref, bf16[1024,1024]{1,0:T(8,128)(2,1)S(1)} %owner_order.1.perm_ref), custom_call_target="tpu_custom_call" | custom-call | flops 4000000000 | bytes 18000000 | tf_op jit(solution)/shard_map/token_blocks/pallas_call | solution.py:243
  141.8 1.3 copy-done
  143.1 7.5 %all-to-all-start.3 = ((bf16[32,32,1024]{2,1,0:T(8,128)(2,1)}), bf16[32,32,1024]{2,1,0:T(8,128)(2,1)S(1)}, u32[]{:S(2)}, u32[]{:S(2)}) async-start(bf16[32,32,1024]{2,1,0:T(8,128)(2,1)} %bitcast.9), calls=%async_computation.3 | async-start | bytes 4194304 | tf_op jit(solution)/shard_map/all_to_all | solution.py:304
  150.6 10.8 %noise_scores.1 = bf16[128,64,128]{2,1,0:T(8,128)(2,1)} custom-call(s32[1]{0:T(128)} %bitcast.base_ref, s32[4]{0:T(128)S(1)} %copy-done.2, bf16[64,432]{1,0:T(8,128)(2,1)S(1)} %subspace.1.pt_ref, bf16[128,432,128]{2,1,0:T(8,128)(2,1)} %get-tuple-element.5.xt_ref.x_ref.next_ref, bf16[128,432,128]{2,1,0:T(8,128)(2,1)} %get-tuple-element.5.xt_ref.x_ref.next_ref, ...), custom_call_target="tpu_custom_call" | custom-call | flops 4000000000 | bytes 18000000 | tf_op jit(solution)/shard_map/noise_scores/pallas_call | solution.py:270
  161.4 17.5 %all-to-all-done.3 = bf16[32,32,1024]{2,1,0:T(8,128)(2,1)S(1)} async-done(((bf16[32,32,1024]{2,1,0:T(8,128)(2,1)}), bf16[32,32,1024]{2,1,0:T(8,128)(2,1)S(1)}, u32[]{:S(2)}, u32[]{:S(2)}) %all-to-all-start.3) | async-done | bytes 2097184 | tf_op jit(solution)/shard_map/all_to_all | solution.py:304
  179.0 1.3 copy.10
  (10 shorter events, 0.1 us)
Async XLA Ops:
  1.9 7.0 %collective-permute-start = (bf16[1,425,128]{2,1,0:T(8,128)(2,1)S(1)}, bf16[1,425,128]{2,1,0:T(8,128)(2,1)S(1)}, u32[]{:S(2)}, u32[]{:S(2)}) collective-permute-start(bf16[1,425,128]{2,1,0:T(8,128)(2,1)S(1)} %copy.8), channel_id=1, source_target_pairs={{4,0},{8,4},{12,8},{16,12},{20,16},{24,20},{28,24},{32,28},{36,32}... | collective-permute-start | bytes 326408 | tf_op jit(solution)/shard_map/ppermute | solution.py:285
  8.9 0.7 copy-start.1
  28.7 25.8 %all-to-all-start = ((f32[128,8,128]{2,1,0:T(8,128)}), f32[128,8,128]{2,1,0:T(8,128)S(1)}, u32[]{:S(2)}, u32[]{:S(2)}) async-start(f32[128,8,128]{2,1,0:T(8,128)} %bitcast.2), calls=%async_computation | async-start | bytes 1048576 | tf_op jit(solution)/shard_map/all_to_all | solution.py:290
  54.7 8.1 %copy-start.5 = (f32[425,64]{0,1:T(8,128)S(1)}, f32[425,64]{0,1:T(8,128)}, u32[]{:S(2)}) copy-start(f32[425,64]{0,1:T(8,128)} %param.7) | copy-start | bytes 326404
  54.7 8.2 %copy-start.6 = (s32[32,32]{1,0:T(8,128)S(1)}, s32[32,32]{1,0:T(8,128)}, u32[]{:S(2)}) copy-start(s32[32,32]{1,0:T(8,128)} %param.6) | copy-start | bytes 12292
  55.8 26.2 %all-to-all-start.1 = ((f32[128,16,128]{2,1,0:T(8,128)}), f32[128,16,128]{2,1,0:T(8,128)}, u32[]{:S(2)}, u32[]{:S(2)}) async-start(f32[128,16,128]{2,1,0:T(8,128)} %pad_maximum_fusion), calls=%async_computation.1 | async-start | bytes 2097152 | tf_op jit(solution)/shard_map/all_to_all | solution.py:295
  84.1 25.7 %all-to-all-start.2 = ((f32[128,8,128]{2,1,0:T(8,128)}), f32[128,8,128]{2,1,0:T(8,128)S(1)}, u32[]{:S(2)}, u32[]{:S(2)}) async-start(f32[128,8,128]{2,1,0:T(8,128)} %broadcast_in_dim.7), calls=%async_computation.2 | async-start | bytes 1048576 | tf_op jit(solution)/shard_map/all_to_all | solution.py:300
  108.9 0.9 copy-start.3
  109.8 1.2 copy-start.4
  141.8 1.3 copy-start
  143.1 7.5 %copy-start.2 = (s32[4]{0:T(128)S(1)}, s32[4]{0:T(128)}, u32[]{:S(2)}) copy-start(s32[4]{0:T(128)} %starts_ref.3) | copy-start | bytes 52
  143.1 35.9 %all-to-all-start.3 = ((bf16[32,32,1024]{2,1,0:T(8,128)(2,1)}), bf16[32,32,1024]{2,1,0:T(8,128)(2,1)S(1)}, u32[]{:S(2)}, u32[]{:S(2)}) async-start(bf16[32,32,1024]{2,1,0:T(8,128)(2,1)} %bitcast.9), calls=%async_computation.3 | async-start | bytes 4194304 | tf_op jit(solution)/shard_map/all_to_all | solution.py:304
where the time goes:
time: 181 us; the launch traced here: 180 us
  Pallas kernels  99.3 us (55%)
  waiting for transfers between devices  36.1 us (20%)
  starting transfers between devices  33.8 us (19%)
  local copies, waits for them, and re-layouts  7.74 us (4%)
  other arithmetic  2.51 us (1%)
    pallas_call x1, Pallas kernels, whiten(): pl.pallas_call(functools.partial(whiten_kernel, norm=norm), out_shape=jax...  20.7 us
    pallas_call x1, Pallas kernels, noise_moments(): pl.pallas_call(noise_kernel, grid_spec=pltpu.PrefetchScalarGridSpec(num_s...  19.1 us
    all_to_all x1, waiting for transfers between devices, local(): lax.all_to_all(outgoing.reshape(OWN, PATCHES // OWN, 1024), 'rows', 0, 0,...  17.5 us
    pallas_call x1, Pallas kernels, subspace(): pl.pallas_call(functools.partial(subspace_kernel, total=total), out_shape...  16.8 us
    pallas_call x1, Pallas kernels, token_blocks(): pl.pallas_call(token_kernel, grid=(128 // R,), in_specs=[pl.BlockSpec((KC...  14 us
    all_to_all x1, starting transfers between devices, local(): lax.all_to_all(noise_part.reshape(TILES, 8, 128), both, 0, 0, tiled=True)  11.9 us
    all_to_all x1, waiting for transfers between devices, local(): mixed = lax.all_to_all(mixed, both, 0, 0, tiled=True)  11.6 us
    pallas_call x1, Pallas kernels, scores(): pl.pallas_call(score_kernel, grid_spec=pltpu.PrefetchScalarGridSpec(num_s...  10.8 us
  transfers between devices with their start and end apart: 5, of which 4 were waited for; matrix products, arithmetic and copies ran while one was open for 0% of the time, Pallas kernels for 27%

commit v1 on v0

v1 whole, which is shorter than its diff:
```python
import functools

import jax
import jax.numpy as jnp
from jax import lax
from jax.experimental import pallas as pl
from jax.experimental.pallas import tpu as pltpu
from jax.sharding import PartitionSpec as P

B = 425
BP = 432
BW = 512
KC = 64
R = 16
OWN = 32
PATCHES = 1024
TILES = 128
F32 = jnp.float32
BF = jnp.bfloat16
NN = (((1,), (0,)), ((), ()))
NT = (((1,), (1,)), ((), ()))


def lower_gram(acc_ref, a):
    nt=(((1,),(1,)),((),()))
    g=lax.dot_general(a, a[0:256], nt, preferred_element_type=jnp.float32)
    h=lax.dot_general(a[256:432], a[256:432], nt, preferred_element_type=jnp.float32)
    acc_ref[0:432,:]+=g[:,0:128]
    acc_ref[432:736,:]+=g[128:432,128:256]
    acc_ref[736:912,:]+=h[:,0:128]
    acc_ref[912:960,0:48]+=h[128:176,128:176]

def kept(base_ref, starts_ref, row):
    nxt=base_ref[0]+row+1
    ok=jnp.logical_and(nxt<4096,row>=0)
    for i in range(4):
        ok=jnp.logical_and(ok, nxt!=starts_ref[i])
    return ok

CHUNK=48

def noise_kernel(base_ref, starts_ref, x_ref, xt_ref, acc_ref, scr, prev, even, odd):
    s=pl.program_id(0); n=pl.num_programs(0)
    @pl.when(s==0)
    def _():
        acc_ref[...]=jnp.zeros_like(acc_ref)
        prev[...]=jnp.zeros_like(prev)
        odd[...]=jnp.zeros_like(odd)
        scr[:,B*8:BP*8,:]=jnp.ones((4,(BP-B)*8,128),jnp.float32)
    for half,(dst,src) in enumerate(((even,odd),(odd,even))):
        lower_gram(acc_ref, src[...])
        keep=[kept(base_ref,starts_ref,s*2*R+half*R+r-1) for r in range(R)]
        for c in range(0,BP,CHUNK):
            top=min(c+CHUNK,B)
            before=prev[c:c+CHUNK,:]
            for g in range(2):
                scr[2*half+g,c*8:top*8,:]=x_ref[c:top,half*16+g*8:half*16+(g+1)*8,:].astype(jnp.float32).reshape((top-c)*8,128)
            for r in range(R):
                cur=scr[2*half+r//8, pl.ds(c*8+r%8,CHUNK,stride=8),:]
                dst[c:c+CHUNK,r*128:(r+1)*128]=jnp.where(keep[r], before-cur, 0.0).astype(jnp.bfloat16)
                xt_ref[half,c:c+CHUNK,r*128:(r+1)*128]=cur.astype(jnp.bfloat16)
                before=cur
            prev[c:c+CHUNK,:]=before
    @pl.when(s==n-1)
    def _():
        lower_gram(acc_ref, odd[...])

def noise_moments(pixels_t, base, starts):
    return pl.pallas_call(noise_kernel,
      grid_spec=pltpu.PrefetchScalarGridSpec(num_scalar_prefetch=2, grid=(128//(2*R),),
        in_specs=[pl.BlockSpec((B,2*R,128),lambda s,*_:(0,s,0))],
        out_specs=[pl.BlockSpec((2,BP,R*128),lambda s,*_:(s,0,0)), pl.BlockSpec((1024,128),lambda s,*_:(0,0))],
        scratch_shapes=[pltpu.VMEM((4,BP*8,128),jnp.float32), pltpu.VMEM((BP,128),jnp.float32)]+[pltpu.VMEM((BP,R*128),jnp.bfloat16)]*2),
      out_shape=[jax.ShapeDtypeStruct((128//R,BP,R*128),jnp.bfloat16), jax.ShapeDtypeStruct((1024,128),jnp.float32)],
      compiler_params=pltpu.CompilerParams(vmem_limit_bytes=48<<20),
      cost_estimate=pl.CostEstimate(flops=6_000_000_000,bytes_accessed=30_000_000,transcendentals=0), name="noise_moments")(base,starts,pixels_t)

def halo_kernel(base_ref, starts_ref, x_ref, halo_ref, part_ref, acc_ref):
    acc_ref[...]=part_ref[...]
    d=x_ref[0,0:B].astype(jnp.float32)-halo_ref[0].astype(jnp.float32)
    d=jnp.where(kept(base_ref,starts_ref,127), d, 0.0)
    d=jnp.concatenate([d,jnp.zeros((BP-B,128),jnp.float32)],0).astype(jnp.bfloat16)
    lower_gram(acc_ref, d)

def halo_moment(banded, halo, part, base, starts):
    return pl.pallas_call(halo_kernel,
      grid_spec=pltpu.PrefetchScalarGridSpec(num_scalar_prefetch=2, grid=(1,),
        in_specs=[pl.BlockSpec((1,BP,128),lambda s,*_:(128//R-1,0,R-1)), pl.BlockSpec((1,B,128),lambda s,*_:(0,0,0)), pl.BlockSpec((1024,128),lambda s,*_:(0,0))],
        out_specs=pl.BlockSpec((1024,128),lambda s,*_:(0,0))),
      out_shape=jax.ShapeDtypeStruct((1024,128),jnp.float32),
      compiler_params=pltpu.CompilerParams(vmem_limit_bytes=62<<20),
      cost_estimate=pl.CostEstimate(flops=50_000_000,bytes_accessed=1_300_000,transcendentals=0), name="halo_moment")(base,starts,banded,halo,part)

AHEAD=3

def signal_kernel(x_hbm, acc_ref, xbuf, sems):
    blocks=128//R
    def fetch(s): return pltpu.make_async_copy(x_hbm.at[s],xbuf.at[s],sems.at[s])
    for s in range(AHEAD): fetch(s).start()
    acc_ref[...]=jnp.zeros_like(acc_ref)
    @pl.loop(0,blocks)
    def _(s):
        fetch(s).wait()
        @pl.when(s+AHEAD<blocks)
        def _(): fetch(s+AHEAD).start()
        lower_gram(acc_ref,xbuf[s])

def signal_moments(xt):
    return pl.pallas_call(signal_kernel,
      in_specs=[pl.BlockSpec(memory_space=pl.ANY)],out_specs=pl.BlockSpec(memory_space=pltpu.VMEM),
      out_shape=jax.ShapeDtypeStruct((1024,128),jnp.float32),
      scratch_shapes=[pltpu.VMEM((128//R,BP,R*128),jnp.bfloat16),pltpu.SemaphoreType.DMA((128//R,))],
      compiler_params=pltpu.CompilerParams(vmem_limit_bytes=56<<20),
      cost_estimate=pl.CostEstimate(flops=6_000_000_000,bytes_accessed=15_000_000,transcendentals=0), name="signal_moments")(xt)

def cut(x):
    hi=x.astype(BF)
    return hi,(x-hi.astype(F32)).astype(BF)

def times(a,b,dims=NN):
    (ah,al),(bh,bl)=a,b
    def mm(x,y): return lax.dot_general(x,y,dims,preferred_element_type=F32)
    return mm(ah,bh)+(mm(ah,bl)+mm(al,bh))

def unpacked(ref, full):
    starts=(0,432,736,912)
    for j in range(4):
        lo=starts[j]; rows=BP-128*j
        full[128*j:BP,128*j:128*(j+1)]=ref[lo:lo+rows,:]
    for j in range(4):
        for i in range(j+1,4):
            full[128*j:128*(j+1),128*i:128*(i+1)]=full[128*i:128*(i+1),128*j:128*(j+1)].T

GROUP=8

def triangular_inverse(g):
    shape=(KC,2*KC)
    row=lax.broadcasted_iota(jnp.int32,shape,0); col=lax.broadcasted_iota(jnp.int32,shape,1)
    m=jnp.concatenate([g,jnp.zeros((KC,KC),F32)],axis=1)+jnp.where(col==row+KC,1.0,0.0)
    for j in range(0,KC,GROUP):
        lines=[m[j+a:j+a+1,:] for a in range(GROUP)]
        cols=[jnp.broadcast_to(m[:,j+a:j+a+1],shape) for a in range(GROUP)]
        roots=[]
        for a in range(GROUP):
            pivot=cols[a][j+a:j+a+1,:]
            inv=1.0/pivot
            roots.append(lax.rsqrt(pivot))
            for b in range(a+1,GROUP):
                f=cols[a][j+b:j+b+1,:]*inv
                lines[b]=lines[b]-f*lines[a]
                cols[b]=cols[b]-cols[a]*f
            cols[a]=cols[a]*inv
        below=row>=j+GROUP
        for a in range(GROUP): m=m-jnp.where(below,cols[a],0.0)*lines[a]
        for a in range(GROUP): m=jnp.where(row==j+a,lines[a]*roots[a],m)
    return m[:,KC:]

def orthonormal(y):
    yc=cut(y)
    yt=y.T
    g=times(cut(yt),yc)
    li=triangular_inverse(g)
    return times(yc,cut(li),NT)

def put(ref,i,x):
    h,l=cut(x)
    ref[i,0,0:BP,:]=h; ref[i,1,0:BP,:]=l
def got(ref,i,rows=BW): return ref[i,0,0:rows,:],ref[i,1,0:rows,:]

def times_symmetric(ref,i,j):
    a=got(ref,i,BP); b=got(ref,j)
    left=times(a,(b[0][:,0:256],b[1][:,0:256]))
    right=times((a[0][256:BP],a[1][256:BP]),(b[0][:,256:BW],b[1][:,256:BW]))
    corner=jnp.concatenate([left[256:BP],jnp.zeros((BW-BP,256),F32)],axis=0).T
    return jnp.concatenate([left,jnp.concatenate([corner,right],axis=0)],axis=1)

def whiten_kernel(n_ref, w_ref, full, cuts, *, norm, pairs):
    full[...]=jnp.zeros_like(full)
    cuts[...]=jnp.zeros_like(cuts)
    unpacked(n_ref, full)
    row=lax.broadcasted_iota(jnp.int32,(BP,BW),0); col=lax.broadcasted_iota(jnp.int32,(BP,BW),1)
    inside=jnp.logical_and(row<B,col<B)
    cov=jnp.where(inside, full[0:BP,:]*(1.0/norm), 0.0)
    scale=jnp.max(jnp.sum(jnp.abs(cov),axis=1,keepdims=True),axis=0,keepdims=True)
    eye=jnp.where(jnp.logical_and(row==col,row<B),1.0,0.0)
    z=cov/scale
    low=None
    for k in range(pairs):
        put(cuts,0,z)
        z2=times_symmetric(cuts,0,0)
        put(cuts,1,z2)
        put(cuts,2,0.0625*z2-0.5625*z)
        q=0.75*eye-2.4375*z+1.6875*z2+times_symmetric(cuts,1,2)
        put(cuts,1,q)
        if low is None: low=q+1.5*eye
        else:
            put(cuts,3,low)
            low=1.5*low+times_symmetric(cuts,1,3)
        if k<pairs-1:
            u=1.5*z+times_symmetric(cuts,0,1)
            put(cuts,2,u)
            z=1.5*u+times_symmetric(cuts,2,1)
    w_ref[...]=low*lax.rsqrt(scale)

def whiten(tiles,norm):
    return pl.pallas_call(functools.partial(whiten_kernel,norm=norm,pairs=5),
      out_shape=jax.ShapeDtypeStruct((BP,BW),F32),
      scratch_shapes=[pltpu.VMEM((BW,BW),F32),pltpu.VMEM((4,2,BW,BW),BF)],
      compiler_params=pltpu.CompilerParams(vmem_limit_bytes=24<<20),
      cost_estimate=pl.CostEstimate(flops=15_000_000_000,bytes_accessed=2_000_000,transcendentals=0),name="whiten")(tiles)

def start_kernel(b_ref,o_ref,pad):
    pad[...]=jnp.zeros_like(pad)
    pad[0:B,:]=b_ref[...]
    o_ref[...]=orthonormal(pad[...])

def start_orth(b):
    return pl.pallas_call(start_kernel,out_shape=jax.ShapeDtypeStruct((BP,KC),F32),scratch_shapes=[pltpu.VMEM((BP,KC),F32)],
      compiler_params=pltpu.CompilerParams(vmem_limit_bytes=40<<20),
      cost_estimate=pl.CostEstimate(flops=100_000_000,bytes_accessed=2_000_000,transcendentals=0),name="start_orth")(b)

def subspace_kernel(s_ref,w_ref,q_ref,pt_ref,full,cuts,thin,*,total):
    full[...]=jnp.zeros_like(full)
    cuts[...]=jnp.zeros_like(cuts)
    thin[...]=jnp.zeros_like(thin)
    unpacked(s_ref,full)
    row=lax.broadcasted_iota(jnp.int32,(BP,BW),0); col=lax.broadcasted_iota(jnp.int32,(BP,BW),1)
    inside=jnp.logical_and(row<B,col<B)
    mrow=full[B:B+1,:]*(1.0/total)
    mcol=full[0:BP,B:B+1]*(1.0/total)
    cov=jnp.where(inside,full[0:BP,:]*(1.0/total)-mcol*mrow,0.0)
    put(cuts,0,cov)
    put(cuts,1,w_ref[...])
    put(cuts,2,times(got(cuts,1,BP),got(cuts,0)))
    put(cuts,0,times(got(cuts,2,BP),got(cuts,1)))
    def thin_cut(x):
        h,l=cut(x); thin[0,0:BP,:]=h; thin[1,0:BP,:]=l
        return thin[0],thin[1]
    q=q_ref[...]
    for _ in range(2):
        q=orthonormal(times(got(cuts,0,BP),thin_cut(q)))
    p=times(got(cuts,1,BP),thin_cut(q)).astype(BF)
    pt=p.astype(F32).T
    off=-jnp.sum(pt*mrow[:,0:BP],axis=1,keepdims=True)
    lane=lax.broadcasted_iota(jnp.int32,(KC,BP),1)
    o1=off.astype(BF).astype(F32); o2=(off-o1).astype(BF).astype(F32); o3=off-o1-o2
    pt=jnp.where(lane<B,pt,jnp.where(lane==B,o1,jnp.where(lane==B+1,o2,jnp.where(lane==B+2,o3,0.0))))
    pt_ref[...]=pt.astype(BF)


def order_kernel(o_ref, perm_ref):
    own=o_ref[...]
    hot=lax.broadcasted_iota(jnp.int32,(OWN,PATCHES),0)==own
    before=(lax.broadcasted_iota(jnp.int32,(PATCHES,PATCHES),0)<lax.broadcasted_iota(jnp.int32,(PATCHES,PATCHES),1))
    rank=lax.dot_general(hot.astype(F32).astype(BF),before.astype(F32).astype(BF),NN,preferred_element_type=F32)
    rank=jnp.sum(jnp.where(hot,rank,0.0),axis=0,keepdims=True)
    place=own*(PATCHES//OWN)+rank.astype(jnp.int32)
    perm_ref[...]=(lax.broadcasted_iota(jnp.int32,(PATCHES,PATCHES),0)==place).astype(F32).astype(BF)

def owner_order(own):
    return pl.pallas_call(order_kernel,out_shape=jax.ShapeDtypeStruct((PATCHES,PATCHES),BF),
      compiler_params=pltpu.CompilerParams(vmem_limit_bytes=40<<20),
      cost_estimate=pl.CostEstimate(flops=100_000_000,bytes_accessed=2_000_000,transcendentals=0),name="owner_order")(own)

def project_kernel(s_ref,w_ref,q_ref,perm_ref,x_hbm,pt_ref,out_ref,full,cuts,thin,tok,xbuf,sems,*,total):
    blocks=128//R
    def fetch(s): return pltpu.make_async_copy(x_hbm.at[s],xbuf.at[s],sems.at[s])
    for s in range(blocks): fetch(s).start()
    subspace_kernel(s_ref,w_ref,q_ref,pt_ref,full,cuts,thin,total=total)
    a=lax.broadcasted_iota(jnp.int32,(128,128),0); c=lax.broadcasted_iota(jnp.int32,(128,128),1)
    pick=((a%32)*4+a//32==c).astype(F32).astype(BF)
    @pl.loop(0,blocks)
    def _(s):
        fetch(s).wait()
        pt=pt_ref[...]
        for p in range(R//4):
            ys=[]
            for h in range(2):
                r=4*p+2*h
                y=lax.dot_general(pt,xbuf[s,:,r*128:(r+2)*128],NN,preferred_element_type=F32).astype(BF)
                ys+=[y[:,0:128],y[:,128:256]]
            y=jnp.concatenate(ys,axis=0)
            t=lax.dot_general(pick,y,NT,preferred_element_type=F32)
            parts=[t[32*j:32*(j+1),64*i:64*(i+1)] for i in range(4) for j in range(4)]
            tok[pl.ds(pl.multiple_of(s*(R//4)*32+p*32,32),32),:]=jnp.concatenate(parts,axis=1).astype(BF)
    for m in range(4):
        out_ref[:,256*m:256*(m+1)]=lax.dot_general(perm_ref[...],tok[:,256*m:256*(m+1)],NN,preferred_element_type=F32).astype(BF)

def project(tiles,w,q,perm,xt,total):
    whole=pl.BlockSpec(memory_space=pltpu.VMEM)
    return pl.pallas_call(functools.partial(project_kernel,total=total),
      in_specs=[whole]*4+[pl.BlockSpec(memory_space=pl.ANY)],out_specs=[whole]*2,
      out_shape=[jax.ShapeDtypeStruct((KC,BP),BF),jax.ShapeDtypeStruct((PATCHES,1024),BF)],
      scratch_shapes=[pltpu.VMEM((BW,BW),F32),pltpu.VMEM((3,2,BW,BW),BF),pltpu.VMEM((2,BW,KC),BF),pltpu.VMEM((PATCHES,1024),BF),
        pltpu.VMEM((128//R,BP,R*128),BF),pltpu.SemaphoreType.DMA((128//R,))],
      compiler_params=pltpu.CompilerParams(vmem_limit_bytes=52<<20),
      cost_estimate=pl.CostEstimate(flops=8_000_000_000,bytes_accessed=18_000_000,transcendentals=0),name="project")(tiles,w,q,perm,xt)

def score_kernel(base_ref,starts_ref,pt_ref,x_ref,next_ref,halo_ref,out_ref):
    s=pl.program_id(0); n=pl.num_programs(0)
    pt=pt_ref[...]
    def differ(r):
        cur=x_ref[0,:,r*128:(r+1)*128].astype(F32)
        if r<R-1: ahead=x_ref[0,:,(r+1)*128:(r+2)*128].astype(F32)
        else:
            halo=jnp.concatenate([halo_ref[0].astype(F32),jnp.ones((BP-B,128),F32)],axis=0)
            ahead=jnp.where(s==n-1,halo,next_ref[0].astype(F32))
        return jnp.where(kept(base_ref,starts_ref,s*R+r),cur-ahead,0.0).astype(BF)
    for h in range(R//2):
        y=lax.dot_general(pt,jnp.concatenate([differ(2*h),differ(2*h+1)],axis=1),NN,preferred_element_type=F32).astype(BF)
        out_ref[2*h]=y[:,0:128]; out_ref[2*h+1]=y[:,128:256]

def scores(pt,xt,halo,base,starts):
    n=128//R
    return pl.pallas_call(score_kernel,
      grid_spec=pltpu.PrefetchScalarGridSpec(num_scalar_prefetch=2,grid=(n,),
        in_specs=[pl.BlockSpec((KC,BP),lambda s,*_:(0,0)),pl.BlockSpec((1,BP,R*128),lambda s,*_:(s,0,0)),
          pl.BlockSpec((1,BP,128),lambda s,*_:(jnp.minimum(s+1,128//R-1),0,0)),pl.BlockSpec((1,B,128),lambda s,*_:(0,0,0))],
        out_specs=pl.BlockSpec((R,KC,128),lambda s,*_:(s,0,0))),
      out_shape=jax.ShapeDtypeStruct((128,KC,128),BF),
      compiler_params=pltpu.CompilerParams(vmem_limit_bytes=63<<20),
      cost_estimate=pl.CostEstimate(flops=4_000_000_000,bytes_accessed=18_000_000,transcendentals=0),name="noise_scores")(base,starts,pt,xt,xt,halo)


def local(pixels, scene_starts, owners, start_basis):
    rows = lax.axis_size("rows")
    cols = lax.axis_size("tok")
    local_rows = pixels.shape[0]
    both = ("rows", "tok")
    halo = lax.ppermute(pixels[0:1], "rows", [(r, r - 1) for r in range(1, rows)])
    base = (lax.axis_index("rows") * local_rows).astype(jnp.int32).reshape(1)
    total = float(rows * local_rows * cols * pixels.shape[2])
    norm = 2.0 * (rows * local_rows - scene_starts.shape[0]) * cols * pixels.shape[2]
    banded, noise_part = noise_moments(jnp.transpose(pixels, (1, 0, 2)), base, scene_starts)
    noise_part = halo_moment(banded, halo, noise_part, base, scene_starts)
    noise_own = lax.all_to_all(noise_part.reshape(TILES, 8, 128), both, 0, 0, tiled=True).sum(axis=0)
    signal_part = signal_moments(banded)
    mixed = jnp.concatenate(
        [jnp.broadcast_to(noise_own, (TILES, 8, 128)), signal_part.reshape(TILES, 8, 128)], axis=1
    )
    mixed = lax.all_to_all(mixed, both, 0, 0, tiled=True)
    noise = mixed[:, 0:8].reshape(TILES * 8, 128)
    signal_own = mixed[:, 8:16].sum(axis=0)
    perm = owner_order(owners.reshape(1, PATCHES))
    basis = start_orth(start_basis)
    signal = lax.all_to_all(jnp.broadcast_to(signal_own, (TILES, 8, 128)), both, 0, 0, tiled=True)
    whitener = whiten(noise, norm)
    projector, outgoing = project(signal.reshape(TILES * 8, 128), whitener, basis, perm, banded, total)
    arrived = lax.all_to_all(outgoing.reshape(OWN, PATCHES // OWN, 1024), "rows", 0, 0, tiled=True)
    noise_scores = scores(projector, banded, halo, base, scene_starts)
    return arrived.reshape(PATCHES, 1024), noise_scores


def solution(mesh):
    return jax.shard_map(
        local,
        mesh=mesh,
        in_specs=(P("rows", None, "tok"), P(), P("rows", "tok"), P()),
        out_specs=(P(("rows", "tok"), None), P("rows", None, "tok")),
        check_vma=False,
    )
```

time: 181 us -> 164 us (0.906)
  Pallas kernels: 99.3 us -> 84.2 us
  starting transfers between devices: 33.8 us -> 30.1 us
    pallas_call x4, Pallas kernels: 62.1 us -> 51.7 us  [the longest x1 23.1 us: project(): pl.pallas_call(functools.partial(project_kernel, total=total), in_specs=[...]
    pallas_call x1, Pallas kernels: 6.03 us -> 2.22 us  [start_orth(): pl.pallas_call(start_kernel, out_shape=jax.ShapeDtypeStruct((BP, KC), F32...]
    ppermute x1, waiting for transfers between devices: 3.71 us -> 0.01 us  [local(): lax.ppermute(pixels[0:1], 'rows', [(r, r - 1) for r in range(1, rows)])]
    all_to_all x1, waiting for transfers between devices: 11.6 us -> 14.4 us  [local(): mixed = lax.all_to_all(mixed, both, 0, 0, tiled=True)]
    all_to_all x1, starting transfers between devices: 6.99 us -> 5.02 us  [local(): mixed = lax.all_to_all(mixed, both, 0, 0, tiled=True)]
  transfers between devices with their start and end apart: 5 -> 5, of which waited for: 4 -> 3; matrix products, arithmetic and copies ran while one was open for 0% -> 0% of each run, Pallas kernels for 27% -> 36%
where the time goes in v1:
time: 164 us
  Pallas kernels  84.2 us (51%)
  waiting for transfers between devices  36.7 us (22%)
  starting transfers between devices  30.1 us (18%)
  local copies, waits for them, and re-layouts  9.47 us (6%)
  other arithmetic  2.39 us (1%)
    pallas_call x1, Pallas kernels, project(): pl.pallas_call(functools.partial(project_kernel, total=total), in_specs=[...  23.1 us
    pallas_call x1, Pallas kernels, noise_moments(): pl.pallas_call(noise_kernel, grid_spec=pltpu.PrefetchScalarGridSpec(num_s...  18 us
    all_to_all x1, waiting for transfers between devices, local(): lax.all_to_all(outgoing.reshape(OWN, PATCHES // OWN, 1024), 'rows', 0, 0,...  17.5 us
    pallas_call x1, Pallas kernels, whiten(): pl.pallas_call(functools.partial(whiten_kernel, norm=norm, pairs=5), out_...  16.6 us
    all_to_all x1, waiting for transfers between devices, local(): mixed = lax.all_to_all(mixed, both, 0, 0, tiled=True)  14.4 us
    pallas_call x1, Pallas kernels, scores(): pl.pallas_call(score_kernel, grid_spec=pltpu.PrefetchScalarGridSpec(num_s...  10.9 us
    all_to_all x1, starting transfers between devices, local(): lax.all_to_all(noise_part.reshape(TILES, 8, 128), both, 0, 0, tiled=True)  10.2 us
    pallas_call x1, Pallas kernels, signal_moments(): pl.pallas_call(signal_kernel, in_specs=[pl.BlockSpec(memory_space=pl.ANY)...  9.14 us
  transfers between devices with their start and end apart: 5, of which 3 were waited for; matrix products, arithmetic and copies ran while one was open for 0% of the time, Pallas kernels for 36%

profile of v1, /device:TPU:1, one launch (start us, length us, event | category | flops | bytes accessed | tf_op | source)
XLA Modules:
  0.0 163.6 jit_solution(15872894052138755323)
XLA Ops:
  0.6 1.3 slice.9
  1.9 3.3 %collective-permute-start = (bf16[1,425,128]{2,1,0:T(8,128)(2,1)S(1)}, bf16[1,425,128]{2,1,0:T(8,128)(2,1)S(1)}, u32[]{:S(2)}, u32[]{:S(2)}) collective-permute-start(bf16[1,425,128]{2,1,0:T(8,128)(2,1)S(1)} %copy.8), channel_id=1, source_target_pairs={{4,0},{8,4},{12,8},{16,12},{20,16},{24,20},{28,24},{32,28},{36,32}... | collective-permute-start | bytes 326408 | tf_op jit(solution)/shard_map/ppermute | solution.py:330
  5.2 0.0 copy-start.3
  5.3 0.6 copy-done.3
  5.9 18.0 %noise_moments.1 = (bf16[8,432,2048]{2,1,0:T(8,128)(2,1)}, f32[1024,128]{1,0:T(8,128)S(1)}) custom-call(s32[1]{0:T(128)} %bitcast.base_ref, s32[4]{0:T(128)S(1)} %copy-done.3, bf16[425,128,128]{2,1,0:T(8,128)(2,1)} %bitcast.13), custom_call_target="tpu_custom_call" | custom-call | flops 6000000000 | bytes 30000000 | tf_op jit(solution)/shard_map/noise_moments/pallas_call | solution.py:69
  23.9 0.8 copy-done.1
  24.7 0.6 copy-done.4
  25.3 2.9 %halo_moment.1 = f32[1024,128]{1,0:T(8,128)} custom-call(s32[1]{0:T(128)} %bitcast.base_ref, s32[4]{0:T(128)} %starts_ref.5, bf16[8,432,2048]{2,1,0:T(8,128)(2,1)} %get-tuple-element.6.x_ref.x_hbm.next_ref, bf16[1,425,128]{2,1,0:T(8,128)(2,1)} %copy-done.4, f32[1024,128]{1,0:T(8,128)} %copy-done.1), custom_call_target="tpu_custom_call" | custom-call | flops 50000000 | bytes 1300000 | tf_op jit(solution)/shard_map/halo_moment/pallas_call | solution.py:86
  28.2 10.2 %all-to-all-start = ((f32[128,8,128]{2,1,0:T(8,128)}), f32[128,8,128]{2,1,0:T(8,128)S(1)}, u32[]{:S(2)}, u32[]{:S(2)}) async-start(f32[128,8,128]{2,1,0:T(8,128)} %bitcast.10), calls=%async_computation | async-start | bytes 1048576 | tf_op jit(solution)/shard_map/all_to_all | solution.py:336
  38.5 9.1 %signal_moments.1 = f32[1024,128]{1,0:T(8,128)} custom-call(bf16[8,432,2048]{2,1,0:T(8,128)(2,1)} %get-tuple-element.6.x_ref.x_hbm.next_ref), custom_call_target="tpu_custom_call" | custom-call | flops 6000000000 | bytes 15000000 | tf_op jit(solution)/shard_map/signal_moments/pallas_call | solution.py:109
  47.6 4.8 %all-to-all-done = f32[128,8,128]{2,1,0:T(8,128)S(1)} async-done(((f32[128,8,128]{2,1,0:T(8,128)}), f32[128,8,128]{2,1,0:T(8,128)S(1)}, u32[]{:S(2)}, u32[]{:S(2)}) %all-to-all-start) | async-done | bytes 524320 | tf_op jit(solution)/shard_map/all_to_all | solution.py:336
  52.4 0.1 reduce_sum.18
  52.6 0.0 copy-start.5
  52.6 2.1 %pad_maximum_fusion = f32[128,16,128]{2,1,0:T(8,128)} fusion(f32[128,8,128]{2,1,0:T(8,128)} %bitcast.12, f32[128,8,128]{2,1,0:T(8,128)S(1)} %broadcast_in_dim.6), kind=kLoop, calls=%fused_computation | loop fusion | flops 262144 | bytes 2097152 | tf_op jit(solution)/shard_map/concatenate | solution.py:338
  54.7 5.0 %all-to-all-start.1 = ((f32[128,16,128]{2,1,0:T(8,128)}), f32[128,16,128]{2,1,0:T(8,128)S(1)}, u32[]{:S(2)}, u32[]{:S(2)}) async-start(f32[128,16,128]{2,1,0:T(8,128)} %pad_maximum_fusion), calls=%async_computation.1 | async-start | bytes 2097152 | tf_op jit(solution)/shard_map/all_to_all | solution.py:341
  59.7 0.1 reshape.33.o_ref
  59.8 0.1 copy.7.b_ref
  59.9 2.2 %start_orth.1.q_ref = f32[432,64]{1,0:T(8,128)S(1)} custom-call(f32[425,64]{1,0:T(8,128)S(1)} %copy.7.b_ref), custom_call_target="tpu_custom_call" | custom-call | flops 100000000 | bytes 2000000 | tf_op jit(solution)/shard_map/start_orth/pallas_call | solution.py:218
  62.2 1.3 owner_order.1.perm_ref
  63.5 0.0 copy-start
  63.5 1.3 copy-done
  64.8 14.4 %all-to-all-done.1 = f32[128,16,128]{2,1,0:T(8,128)S(1)} async-done(((f32[128,16,128]{2,1,0:T(8,128)}), f32[128,16,128]{2,1,0:T(8,128)S(1)}, u32[]{:S(2)}, u32[]{:S(2)}) %all-to-all-start.1) | async-done | bytes 1048608 | tf_op jit(solution)/shard_map/all_to_all | solution.py:341
  79.2 0.1 slice_bitcast_fusion
  79.4 0.8 broadcast_in_dim.7
  80.2 4.1 %all-to-all-start.2 = ((f32[128,8,128]{2,1,0:T(8,128)}), f32[128,8,128]{2,1,0:T(8,128)S(1)}, u32[]{:S(2)}, u32[]{:S(2)}) async-start(f32[128,8,128]{2,1,0:T(8,128)} %broadcast_in_dim.7), calls=%async_computation.2 | async-start | bytes 1048576 | tf_op jit(solution)/shard_map/all_to_all | solution.py:346
  84.3 16.6 %whiten.1.w_ref = f32[432,512]{1,0:T(8,128)S(1)} custom-call(f32[1024,128]{1,0:T(8,128)S(1)} %get-tuple-element.10.n_ref), custom_call_target="tpu_custom_call" | custom-call | flops 15000000512 | bytes 2000000 | tf_op jit(solution)/shard_map/whiten/pallas_call | solution.py:206
  100.9 23.1 %project.1 = (bf16[64,432]{1,0:T(8,128)(2,1)S(1)}, bf16[1024,1024]{1,0:T(8,128)(2,1)}) custom-call(f32[1024,128]{1,0:T(8,128)S(1)} %bitcast.9, f32[432,512]{1,0:T(8,128)S(1)} %whiten.1.w_ref, f32[432,64]{1,0:T(8,128)S(1)} %start_orth.1.q_ref, bf16[1024,1024]{1,0:T(8,128)(2,1)} %copy-done, bf16[8,432,2048]{2,1,0:T(8,128)(2,1)} %get-tuple-element.6.x_ref.x_hbm.next_ref), custom_call_target="tpu_custom_call" | custom-call | flops 8000000000 | bytes 18000000 | tf_op jit(solution)/shard_map/project/pallas_call | solution.py:291
  124.0 0.6 copy-done.2
  124.6 7.4 %all-to-all-start.3 = ((bf16[32,32,1024]{2,1,0:T(8,128)(2,1)}), bf16[32,32,1024]{2,1,0:T(8,128)(2,1)}, u32[]{:S(2)}, u32[]{:S(2)}) async-start(bf16[32,32,1024]{2,1,0:T(8,128)(2,1)} %bitcast.11), calls=%async_computation.3 | async-start | bytes 4194304 | tf_op jit(solution)/shard_map/all_to_all | solution.py:349
  132.1 10.9 %noise_scores.1 = bf16[128,64,128]{2,1,0:T(8,128)(2,1)} custom-call(s32[1]{0:T(128)} %bitcast.base_ref, s32[4]{0:T(128)} %starts_ref.5, bf16[64,432]{1,0:T(8,128)(2,1)} %copy-done.2, bf16[8,432,2048]{2,1,0:T(8,128)(2,1)} %get-tuple-element.6.x_ref.x_hbm.next_ref, bf16[8,432,2048]{2,1,0:T(8,128)(2,1)} %get-tuple-element.6.x_ref.x_hbm.next_ref, ...), custom_call_target="tpu_custom_call" | custom-call | flops 4000000000 | bytes 18000000 | tf_op jit(solution)/shard_map/noise_scores/pallas_call | solution.py:315
  143.0 17.5 %all-to-all-done.3 = bf16[32,32,1024]{2,1,0:T(8,128)(2,1)} async-done(((bf16[32,32,1024]{2,1,0:T(8,128)(2,1)}), bf16[32,32,1024]{2,1,0:T(8,128)(2,1)}, u32[]{:S(2)}, u32[]{:S(2)}) %all-to-all-start.3) | async-done | bytes 2097184 | tf_op jit(solution)/shard_map/all_to_all | solution.py:349
  160.5 3.1 %copy.10 = bf16[1024,1024]{1,0:T(8,128)(2,1)} copy(bf16[1024,1024]{1,0:T(8,128)(2,1)} %bitcast.7) | data formatting | bytes 4194304
  (10 shorter events, 0.1 us)
Async XLA Ops:
  1.9 22.8 %collective-permute-start = (bf16[1,425,128]{2,1,0:T(8,128)(2,1)S(1)}, bf16[1,425,128]{2,1,0:T(8,128)(2,1)S(1)}, u32[]{:S(2)}, u32[]{:S(2)}) collective-permute-start(bf16[1,425,128]{2,1,0:T(8,128)(2,1)S(1)} %copy.8), channel_id=1, source_target_pairs={{4,0},{8,4},{12,8},{16,12},{20,16},{24,20},{28,24},{32,28},{36,32}... | collective-permute-start | bytes 326408 | tf_op jit(solution)/shard_map/ppermute | solution.py:330
  5.2 0.7 copy-start.3
  23.9 0.8 copy-start.1
  24.7 0.6 copy-start.4
  28.2 24.1 %all-to-all-start = ((f32[128,8,128]{2,1,0:T(8,128)}), f32[128,8,128]{2,1,0:T(8,128)S(1)}, u32[]{:S(2)}, u32[]{:S(2)}) async-start(f32[128,8,128]{2,1,0:T(8,128)} %bitcast.10), calls=%async_computation | async-start | bytes 1048576 | tf_op jit(solution)/shard_map/all_to_all | solution.py:336
  52.5 7.2 %copy-start.6 = (s32[32,32]{1,0:T(8,128)S(1)}, s32[32,32]{1,0:T(8,128)}, u32[]{:S(2)}) copy-start(s32[32,32]{1,0:T(8,128)} %param.6) | copy-start | bytes 12292
  52.6 7.2 %copy-start.5 = (f32[425,64]{0,1:T(8,128)S(1)}, f32[425,64]{0,1:T(8,128)}, u32[]{:S(2)}) copy-start(f32[425,64]{0,1:T(8,128)} %param.7) | copy-start | bytes 326404
  54.7 24.6 %all-to-all-start.1 = ((f32[128,16,128]{2,1,0:T(8,128)}), f32[128,16,128]{2,1,0:T(8,128)S(1)}, u32[]{:S(2)}, u32[]{:S(2)}) async-start(f32[128,16,128]{2,1,0:T(8,128)} %pad_maximum_fusion), calls=%async_computation.1 | async-start | bytes 2097152 | tf_op jit(solution)/shard_map/all_to_all | solution.py:341
  63.5 1.3 copy-start
  80.2 20.7 %all-to-all-start.2 = ((f32[128,8,128]{2,1,0:T(8,128)}), f32[128,8,128]{2,1,0:T(8,128)S(1)}, u32[]{:S(2)}, u32[]{:S(2)}) async-start(f32[128,8,128]{2,1,0:T(8,128)} %broadcast_in_dim.7), calls=%async_computation.2 | async-start | bytes 1048576 | tf_op jit(solution)/shard_map/all_to_all | solution.py:346
  124.0 0.6 copy-start.2
  124.6 35.8 %all-to-all-start.3 = ((bf16[32,32,1024]{2,1,0:T(8,128)(2,1)}), bf16[32,32,1024]{2,1,0:T(8,128)(2,1)}, u32[]{:S(2)}, u32[]{:S(2)}) async-start(bf16[32,32,1024]{2,1,0:T(8,128)(2,1)} %bitcast.11), calls=%async_computation.3 | async-start | bytes 4194304 | tf_op jit(solution)/shard_map/all_to_all | solution.py:349

commit v2 on v1

--- a/solution.py
+++ b/solution.py
@@ -72,7 +72,7 @@
         out_specs=[pl.BlockSpec((2,BP,R*128),lambda s,*_:(s,0,0)), pl.BlockSpec((1024,128),lambda s,*_:(0,0))],
         scratch_shapes=[pltpu.VMEM((4,BP*8,128),jnp.float32), pltpu.VMEM((BP,128),jnp.float32)]+[pltpu.VMEM((BP,R*128),jnp.bfloat16)]*2),
       out_shape=[jax.ShapeDtypeStruct((128//R,BP,R*128),jnp.bfloat16), jax.ShapeDtypeStruct((1024,128),jnp.float32)],
-      compiler_params=pltpu.CompilerParams(vmem_limit_bytes=48<<20),
+      compiler_params=pltpu.CompilerParams(vmem_limit_bytes=63<<20),
       cost_estimate=pl.CostEstimate(flops=6_000_000_000,bytes_accessed=30_000_000,transcendentals=0), name="noise_moments")(base,starts,pixels_t)
 
 def halo_kernel(base_ref, starts_ref, x_ref, halo_ref, part_ref, acc_ref):
@@ -88,7 +88,7 @@
         in_specs=[pl.BlockSpec((1,BP,128),lambda s,*_:(128//R-1,0,R-1)), pl.BlockSpec((1,B,128),lambda s,*_:(0,0,0)), pl.BlockSpec((1024,128),lambda s,*_:(0,0))],
         out_specs=pl.BlockSpec((1024,128),lambda s,*_:(0,0))),
       out_shape=jax.ShapeDtypeStruct((1024,128),jnp.float32),
-      compiler_params=pltpu.CompilerParams(vmem_limit_bytes=62<<20),
+      compiler_params=pltpu.CompilerParams(vmem_limit_bytes=53<<20),
       cost_estimate=pl.CostEstimate(flops=50_000_000,bytes_accessed=1_300_000,transcendentals=0), name="halo_moment")(base,starts,banded,halo,part)
 
 AHEAD=3
@@ -110,7 +110,7 @@
       in_specs=[pl.BlockSpec(memory_space=pl.ANY)],out_specs=pl.BlockSpec(memory_space=pltpu.VMEM),
       out_shape=jax.ShapeDtypeStruct((1024,128),jnp.float32),
       scratch_shapes=[pltpu.VMEM((128//R,BP,R*128),jnp.bfloat16),pltpu.SemaphoreType.DMA((128//R,))],
-      compiler_params=pltpu.CompilerParams(vmem_limit_bytes=56<<20),
+      compiler_params=pltpu.CompilerParams(vmem_limit_bytes=53<<20),
       cost_estimate=pl.CostEstimate(flops=6_000_000_000,bytes_accessed=15_000_000,transcendentals=0), name="signal_moments")(xt)
 
 def cut(x):
@@ -267,21 +267,24 @@
     def fetch(s): return pltpu.make_async_copy(x_hbm.at[s],xbuf.at[s],sems.at[s])
     for s in range(blocks): fetch(s).start()
     subspace_kernel(s_ref,w_ref,q_ref,pt_ref,full,cuts,thin,total=total)
-    a=lax.broadcasted_iota(jnp.int32,(128,128),0); c=lax.broadcasted_iota(jnp.int32,(128,128),1)
-    pick=((a%32)*4+a//32==c).astype(F32).astype(BF)
+    a=lax.broadcasted_iota(jnp.int32,(64,256),0); c=lax.broadcasted_iota(jnp.int32,(64,256),1)
+    pick=((a%32)*4+a//32*2+c//128==c%128).astype(F32).astype(BF)
+    none=jnp.zeros((KC,128),BF)
     @pl.loop(0,blocks)
     def _(s):
         fetch(s).wait()
         pt=pt_ref[...]
         for p in range(R//4):
-            ys=[]
+            parts=[]
             for h in range(2):
                 r=4*p+2*h
                 y=lax.dot_general(pt,xbuf[s,:,r*128:(r+2)*128],NN,preferred_element_type=F32).astype(BF)
-                ys+=[y[:,0:128],y[:,128:256]]
-            y=jnp.concatenate(ys,axis=0)
-            t=lax.dot_general(pick,y,NT,preferred_element_type=F32)
-            parts=[t[32*j:32*(j+1),64*i:64*(i+1)] for i in range(4) for j in range(4)]
+                rows=[]
+                for i in range(2):
+                    yi=y[:,128*i:128*(i+1)]
+                    rows+=[jnp.concatenate([yi,none],axis=1),jnp.concatenate([none,yi],axis=1)]
+                t=lax.dot_general(pick,jnp.concatenate(rows,axis=0),NT,preferred_element_type=F32)
+                parts+=[t[32*g:32*(g+1),128*i:128*(i+1)] for i in range(2) for g in range(2)]
             tok[pl.ds(pl.multiple_of(s*(R//4)*32+p*32,32),32),:]=jnp.concatenate(parts,axis=1).astype(BF)
     for m in range(4):
         out_ref[:,256*m:256*(m+1)]=lax.dot_general(perm_ref[...],tok[:,256*m:256*(m+1)],NN,preferred_element_type=F32).astype(BF)
@@ -318,7 +321,7 @@
           pl.BlockSpec((1,BP,128),lambda s,*_:(jnp.minimum(s+1,128//R-1),0,0)),pl.BlockSpec((1,B,128),lambda s,*_:(0,0,0))],
         out_specs=pl.BlockSpec((R,KC,128),lambda s,*_:(s,0,0))),
       out_shape=jax.ShapeDtypeStruct((128,KC,128),BF),
-      compiler_params=pltpu.CompilerParams(vmem_limit_bytes=63<<20),
+      compiler_params=pltpu.CompilerParams(vmem_limit_bytes=48<<20),
       cost_estimate=pl.CostEstimate(flops=4_000_000_000,bytes_accessed=18_000_000,transcendentals=0),name="noise_scores")(base,starts,pt,xt,xt,halo)
 
 

time: 164 us -> 157 us (0.957)
  local copies, waits for them, and re-layouts: 9.47 us -> 5.02 us
    unnamed x17 -> x11, local copies, waits for them, and re-layouts: 7.25 us -> 2.79 us
  transfers between devices with their start and end apart: 5 -> 5, of which waited for: 3 -> 3; matrix products, arithmetic and copies ran while one was open for 0% -> 0% of each run, Pallas kernels for 36% -> 37%
where the time goes in v2:
time: 157 us
  Pallas kernels  82.8 us (53%)
  waiting for transfers between devices  37.5 us (24%)
  starting transfers between devices  29.3 us (19%)
  local copies, waits for them, and re-layouts  5.02 us (3%)
    pallas_call x1, Pallas kernels, project(): pl.pallas_call(functools.partial(project_kernel, total=total), in_specs=[...  22.3 us
    pallas_call x1, Pallas kernels, noise_moments(): pl.pallas_call(noise_kernel, grid_spec=pltpu.PrefetchScalarGridSpec(num_s...  18.4 us
    all_to_all x1, waiting for transfers between devices, local(): lax.all_to_all(outgoing.reshape(OWN, PATCHES // OWN, 1024), 'rows', 0, 0,...  17.6 us
    pallas_call x1, Pallas kernels, whiten(): pl.pallas_call(functools.partial(whiten_kernel, norm=norm, pairs=5), out_...  16.6 us
    all_to_all x1, waiting for transfers between devices, local(): mixed = lax.all_to_all(mixed, both, 0, 0, tiled=True)  14.4 us
    pallas_call x1, Pallas kernels, scores(): pl.pallas_call(score_kernel, grid_spec=pltpu.PrefetchScalarGridSpec(num_s...  10.8 us
    all_to_all x1, starting transfers between devices, local(): lax.all_to_all(noise_part.reshape(TILES, 8, 128), both, 0, 0, tiled=True)  10.2 us
    pallas_call x1, Pallas kernels, signal_moments(): pl.pallas_call(signal_kernel, in_specs=[pl.BlockSpec(memory_space=pl.ANY)...  8.42 us
  transfers between devices with their start and end apart: 5, of which 3 were waited for; matrix products, arithmetic and copies ran while one was open for 0% of the time, Pallas kernels for 37%

profile of v2, /device:TPU:1, one launch (start us, length us, event | category | flops | bytes accessed | tf_op | source)
XLA Modules:
  0.0 156.6 jit_solution(2032228329500092514)
XLA Ops:
  0.6 1.3 slice.9
  1.9 3.3 %collective-permute-start = (bf16[1,425,128]{2,1,0:T(8,128)(2,1)S(1)}, bf16[1,425,128]{2,1,0:T(8,128)(2,1)S(1)}, u32[]{:S(2)}, u32[]{:S(2)}) collective-permute-start(bf16[1,425,128]{2,1,0:T(8,128)(2,1)S(1)} %copy.8), channel_id=1, source_target_pairs={{4,0},{8,4},{12,8},{16,12},{20,16},{24,20},{28,24},{32,28},{36,32}... | collective-permute-start | bytes 326408 | tf_op jit(solution)/shard_map/ppermute | solution.py:333
  5.2 0.0 copy-start.1
  5.3 18.4 %noise_moments.1 = (bf16[8,432,2048]{2,1,0:T(8,128)(2,1)}, f32[1024,128]{1,0:T(8,128)}) custom-call(s32[1]{0:T(128)} %bitcast.base_ref, s32[4]{0:T(128)} %starts_ref.5, bf16[425,128,128]{2,1,0:T(8,128)(2,1)} %bitcast.13), custom_call_target="tpu_custom_call" | custom-call | flops 6000000000 | bytes 30000000 | tf_op jit(solution)/shard_map/noise_moments/pallas_call | solution.py:69
  23.7 0.0 collective-permute-done.halo_ref
  23.7 2.7 %halo_moment.1 = f32[1024,128]{1,0:T(8,128)} custom-call(s32[1]{0:T(128)} %bitcast.base_ref, s32[4]{0:T(128)S(1)} %copy-done.1, bf16[8,432,2048]{2,1,0:T(8,128)(2,1)} %get-tuple-element.6.x_ref.x_hbm.next_ref, bf16[1,425,128]{2,1,0:T(8,128)(2,1)S(1)} %collective-permute-done.halo_ref, f32[1024,128]{1,0:T(8,128)} %get-tuple-element.7.part_ref), custom_call_target="tpu_custom_call" | custom-call | flops 50000000 | bytes 1300000 | tf_op jit(solution)/shard_map/halo_moment/pallas_call | solution.py:86
  26.4 10.2 %all-to-all-start = ((f32[128,8,128]{2,1,0:T(8,128)}), f32[128,8,128]{2,1,0:T(8,128)S(1)}, u32[]{:S(2)}, u32[]{:S(2)}) async-start(f32[128,8,128]{2,1,0:T(8,128)} %bitcast.2), calls=%async_computation | async-start | bytes 1048576 | tf_op jit(solution)/shard_map/all_to_all | solution.py:339
  36.6 8.4 %signal_moments.1 = f32[1024,128]{1,0:T(8,128)S(1)} custom-call(bf16[8,432,2048]{2,1,0:T(8,128)(2,1)} %get-tuple-element.6.x_ref.x_hbm.next_ref), custom_call_target="tpu_custom_call" | custom-call | flops 6000000000 | bytes 15000000 | tf_op jit(solution)/shard_map/signal_moments/pallas_call | solution.py:109
  45.0 5.5 %all-to-all-done = f32[128,8,128]{2,1,0:T(8,128)S(1)} async-done(((f32[128,8,128]{2,1,0:T(8,128)}), f32[128,8,128]{2,1,0:T(8,128)S(1)}, u32[]{:S(2)}, u32[]{:S(2)}) %all-to-all-start) | async-done | bytes 524320 | tf_op jit(solution)/shard_map/all_to_all | solution.py:339
  50.5 0.1 reduce_sum.18
  50.7 0.0 copy-start.3
  50.7 0.0 copy-start.2
  50.7 1.0 pad_maximum_fusion
  51.8 4.3 %all-to-all-start.1 = ((f32[128,16,128]{2,1,0:T(8,128)}), f32[128,16,128]{2,1,0:T(8,128)S(1)}, u32[]{:S(2)}, u32[]{:S(2)}) async-start(f32[128,16,128]{2,1,0:T(8,128)} %pad_maximum_fusion), calls=%async_computation.1 | async-start | bytes 2097152 | tf_op jit(solution)/shard_map/all_to_all | solution.py:344
  56.1 0.0 copy-done.3
  56.1 0.1 reshape.33.o_ref
  56.2 0.1 copy.7.b_ref
  56.3 2.2 %start_orth.1.q_ref = f32[432,64]{1,0:T(8,128)S(1)} custom-call(f32[425,64]{1,0:T(8,128)S(1)} %copy.7.b_ref), custom_call_target="tpu_custom_call" | custom-call | flops 100000000 | bytes 2000000 | tf_op jit(solution)/shard_map/start_orth/pallas_call | solution.py:218
  58.5 1.3 owner_order.1.perm_ref
  59.8 0.0 copy-start
  59.8 1.3 copy-done
  61.1 14.4 %all-to-all-done.1 = f32[128,16,128]{2,1,0:T(8,128)S(1)} async-done(((f32[128,16,128]{2,1,0:T(8,128)}), f32[128,16,128]{2,1,0:T(8,128)S(1)}, u32[]{:S(2)}, u32[]{:S(2)}) %all-to-all-start.1) | async-done | bytes 1048608 | tf_op jit(solution)/shard_map/all_to_all | solution.py:344
  75.6 0.1 slice_bitcast_fusion
  75.7 0.8 broadcast_in_dim.7
  76.6 4.1 %all-to-all-start.2 = ((f32[128,8,128]{2,1,0:T(8,128)}), f32[128,8,128]{2,1,0:T(8,128)S(1)}, u32[]{:S(2)}, u32[]{:S(2)}) async-start(f32[128,8,128]{2,1,0:T(8,128)} %broadcast_in_dim.7), calls=%async_computation.2 | async-start | bytes 1048576 | tf_op jit(solution)/shard_map/all_to_all | solution.py:349
  80.7 16.6 %whiten.1.w_ref = f32[432,512]{1,0:T(8,128)S(1)} custom-call(f32[1024,128]{1,0:T(8,128)S(1)} %get-tuple-element.10.n_ref), custom_call_target="tpu_custom_call" | custom-call | flops 15000000512 | bytes 2000000 | tf_op jit(solution)/shard_map/whiten/pallas_call | solution.py:206
  97.2 0.0 all-to-all-done.2
  97.2 22.3 %project.1 = (bf16[64,432]{1,0:T(8,128)(2,1)S(1)}, bf16[1024,1024]{1,0:T(8,128)(2,1)}) custom-call(f32[1024,128]{1,0:T(8,128)S(1)} %bitcast.9, f32[432,512]{1,0:T(8,128)S(1)} %whiten.1.w_ref, f32[432,64]{1,0:T(8,128)S(1)} %start_orth.1.q_ref, bf16[1024,1024]{1,0:T(8,128)(2,1)} %copy-done, bf16[8,432,2048]{2,1,0:T(8,128)(2,1)} %get-tuple-element.6.x_ref.x_hbm.next_ref), custom_call_target="tpu_custom_call" | custom-call | flops 8000000000 | bytes 18000000 | tf_op jit(solution)/shard_map/project/pallas_call | solution.py:294
  119.6 7.4 %all-to-all-start.3 = ((bf16[32,32,1024]{2,1,0:T(8,128)(2,1)}), bf16[32,32,1024]{2,1,0:T(8,128)(2,1)S(1)}, u32[]{:S(2)}, u32[]{:S(2)}) async-start(bf16[32,32,1024]{2,1,0:T(8,128)(2,1)} %bitcast.12), calls=%async_computation.3 | async-start | bytes 4194304 | tf_op jit(solution)/shard_map/all_to_all | solution.py:352
  127.0 10.8 %noise_scores.1 = bf16[128,64,128]{2,1,0:T(8,128)(2,1)} custom-call(s32[1]{0:T(128)} %bitcast.base_ref, s32[4]{0:T(128)S(1)} %copy-done.1, bf16[64,432]{1,0:T(8,128)(2,1)S(1)} %get-tuple-element.9.pt_ref, bf16[8,432,2048]{2,1,0:T(8,128)(2,1)} %get-tuple-element.6.x_ref.x_hbm.next_ref, bf16[8,432,2048]{2,1,0:T(8,128)(2,1)} %get-tuple-element.6.x_ref.x_hbm.next_ref, ...), custom_call_target="tpu_custom_call" | custom-call | flops 4000000000 | bytes 18000000 | tf_op jit(solution)/shard_map/noise_scores/pallas_call | solution.py:318
  137.8 17.6 %all-to-all-done.3 = bf16[32,32,1024]{2,1,0:T(8,128)(2,1)S(1)} async-done(((bf16[32,32,1024]{2,1,0:T(8,128)(2,1)}), bf16[32,32,1024]{2,1,0:T(8,128)(2,1)S(1)}, u32[]{:S(2)}, u32[]{:S(2)}) %all-to-all-start.3) | async-done | bytes 2097184 | tf_op jit(solution)/shard_map/all_to_all | solution.py:352
  155.3 1.3 copy.10
  (4 shorter events, 0.1 us)
Async XLA Ops:
  1.9 21.7 %collective-permute-start = (bf16[1,425,128]{2,1,0:T(8,128)(2,1)S(1)}, bf16[1,425,128]{2,1,0:T(8,128)(2,1)S(1)}, u32[]{:S(2)}, u32[]{:S(2)}) collective-permute-start(bf16[1,425,128]{2,1,0:T(8,128)(2,1)S(1)} %copy.8), channel_id=1, source_target_pairs={{4,0},{8,4},{12,8},{16,12},{20,16},{24,20},{28,24},{32,28},{36,32}... | collective-permute-start | bytes 326408 | tf_op jit(solution)/shard_map/ppermute | solution.py:333
  5.2 18.4 %copy-start.1 = (s32[4]{0:T(128)S(1)}, s32[4]{0:T(128)}, u32[]{:S(2)}) copy-start(s32[4]{0:T(128)} %starts_ref.5) | copy-start | bytes 52
  26.4 24.1 %all-to-all-start = ((f32[128,8,128]{2,1,0:T(8,128)}), f32[128,8,128]{2,1,0:T(8,128)S(1)}, u32[]{:S(2)}, u32[]{:S(2)}) async-start(f32[128,8,128]{2,1,0:T(8,128)} %bitcast.2), calls=%async_computation | async-start | bytes 1048576 | tf_op jit(solution)/shard_map/all_to_all | solution.py:339
  50.7 5.4 %copy-start.3 = (s32[32,32]{1,0:T(8,128)S(1)}, s32[32,32]{1,0:T(8,128)}, u32[]{:S(2)}) copy-start(s32[32,32]{1,0:T(8,128)} %param.6) | copy-start | bytes 12292
  50.7 5.4 %copy-start.2 = (f32[425,64]{0,1:T(8,128)S(1)}, f32[425,64]{0,1:T(8,128)}, u32[]{:S(2)}) copy-start(f32[425,64]{0,1:T(8,128)} %param.7) | copy-start | bytes 326404
  51.8 23.8 %all-to-all-start.1 = ((f32[128,16,128]{2,1,0:T(8,128)}), f32[128,16,128]{2,1,0:T(8,128)S(1)}, u32[]{:S(2)}, u32[]{:S(2)}) async-start(f32[128,16,128]{2,1,0:T(8,128)} %pad_maximum_fusion), calls=%async_computation.1 | async-start | bytes 2097152 | tf_op jit(solution)/shard_map/all_to_all | solution.py:344
  59.8 1.3 copy-start
  76.6 20.7 %all-to-all-start.2 = ((f32[128,8,128]{2,1,0:T(8,128)}), f32[128,8,128]{2,1,0:T(8,128)S(1)}, u32[]{:S(2)}, u32[]{:S(2)}) async-start(f32[128,8,128]{2,1,0:T(8,128)} %broadcast_in_dim.7), calls=%async_computation.2 | async-start | bytes 1048576 | tf_op jit(solution)/shard_map/all_to_all | solution.py:349
  119.6 35.8 %all-to-all-start.3 = ((bf16[32,32,1024]{2,1,0:T(8,128)(2,1)}), bf16[32,32,1024]{2,1,0:T(8,128)(2,1)S(1)}, u32[]{:S(2)}, u32[]{:S(2)}) async-start(bf16[32,32,1024]{2,1,0:T(8,128)(2,1)} %bitcast.12), calls=%async_computation.3 | async-start | bytes 4194304 | tf_op jit(solution)/shard_map/all_to_all | solution.py:352
